TPU v7x, 256 devices: a whole 4x4x8 slice. The times are simulated.
256 devices in a mesh: seg: 8 (over x, z_lo), bond: 32 (over z_hi, y, core).
Axes of the slice: x: 4, y: 4, z: 8 (z_hi: 4, z_lo: 2; z = z_hi * 2 + z_lo), core: 2. Of those that a mesh axis runs over, the one named last changes fastest.
Arguments:
- last_sites: bfloat16 [8, 1024, 2048], P('seg', 'bond'), may hold values from -6 to 6
- first_sites: bfloat16 [8, 1024, 2048], P('seg', 'bond'), may hold values from -0.1875 to 0.1875
- start_basis: float32 [2048, 256], replicated, may hold values from -6 to 6
- fields: float32 [8, 2], replicated, may hold values from -3 to 3
- ranks: int32 [8], replicated, may hold values from 128 to 256
Outputs:
- new_left: float32 [8, 2048, 256], P('seg', 'bond')
- new_right: float32 [8, 256, 2048], P('seg')
All inputs are finite; a program needn't handle non-finite values.
Results may differ from a plain program's by a relative error of at most 0.00035.
Values may be sent and summed in bfloat16 or wider, within the bound.
A program may use at most 64 MiB of HBM per device.

v0:
```python
import jax
import jax.numpy as jnp
from jax import lax
from jax.sharding import Mesh
from jax.sharding import PartitionSpec as P

ITERS = 4
BOND = ("bond_0", "bond_1", "bond_2")
time_step = 0.5
anisotropy = 0.6


def padded_to(lines, peers):
    spare = -len(lines) % peers
    return jnp.pad(lines, [(0, spare)] + [(0, 0)] * (lines.ndim - 1))


def sent_to_all(x, axis):
    peers = lax.axis_size(axis)
    return lax.all_to_all(jnp.broadcast_to(x[None], (peers, *x.shape)), axis, 0, 0, tiled=True)


def laid_out(pieces, dim):
    pieces = jnp.moveaxis(pieces, 0, dim)
    lengths = pieces.shape
    return pieces.reshape(*lengths[:dim], lengths[dim] * lengths[dim + 1], *lengths[dim + 2 :])


def gathered_by_axis(x, axes, dim):
    far, near = axes
    initial = sent_to_all(x, far)
    pieces = jnp.swapaxes(sent_to_all(initial, near), 0, 1)
    return laid_out(pieces.reshape(-1, *x.shape), dim)


def split_up(x, dim, peers):
    before, after = (x.shape[:dim], x.shape[dim + 1 :])
    return jnp.moveaxis(x.reshape(*before, peers, -1, *after), dim, 0)


def sent_and_summed(x, axis, dim):
    peers = lax.axis_size(axis)
    pieces = lax.all_to_all(split_up(x, dim, peers), axis, 0, 0, tiled=True)
    return jnp.sum(pieces, axis=0)


def sum_by_axis(x, axes, dim):
    far, near = axes
    pieces = split_up(x, dim, lax.axis_size(far))
    nearer = sent_and_summed(pieces, near, dim + 1)
    arrived = lax.all_to_all(nearer, far, split_axis=0, concat_axis=0, tiled=True)
    return arrived.sum(axis=0)


def sum_by_parts(x, axes):
    lines = x.reshape(-1, x.shape[-1])
    padded = padded_to(lines, lax.axis_size(axes[0]) * lax.axis_size(axes[1]))
    whole = gathered_by_axis(sum_by_axis(padded, axes, 0), axes, 0)
    return lax.slice_in_dim(whole, 0, len(lines)).reshape(x.shape)


def passed_along(x, axis, by):
    peers = lax.axis_size(axis)
    return lax.ppermute(x, axis, [(i, (i + by) % peers) for i in range(peers)])


def bond_gate(pair):
    left_field = pair[0]
    right_field = pair[1]
    half_diff = 0.5 * (left_field - right_field)
    width = jnp.sqrt(half_diff * half_diff + 0.25)
    factor = jnp.exp(time_step * anisotropy / 4.0)
    cosine = jnp.cosh(time_step * width)
    ratio = jnp.sinh(time_step * width) / width
    total = left_field + right_field
    zero = jnp.zeros((), jnp.float32)
    first = jnp.exp(-time_step * (anisotropy / 4.0 + total / 2.0))
    last = jnp.exp(-time_step * (anisotropy / 4.0 - total / 2.0))
    middle = factor * (cosine - half_diff * ratio)
    other = factor * (cosine + half_diff * ratio)
    cross = -factor * ratio * 0.5
    rows = [
        jnp.stack([first, zero, zero, zero]),
        jnp.stack([zero, middle, cross, zero]),
        jnp.stack([zero, cross, other, zero]),
        jnp.stack([zero, zero, zero, last]),
    ]
    return jnp.stack(rows).reshape(2, 2, 2, 2)


def apply_gate(theta, pair):
    gate = bond_gate(pair)
    rows = theta.shape[0] // 2
    width = theta.shape[1] // 2
    four = theta.reshape(rows, 2, 2, width)
    mixed = jnp.einsum("pqrs,arsc->apqc", gate, four, precision=lax.Precision.HIGHEST)
    return mixed.reshape(rows * 2, width * 2)


def truncate(left, right, start_basis, pair, rank):
    local_rows = left.shape[0]
    bond_width = right.shape[1] // 2
    left_three = left.reshape(local_rows, 2, bond_width)
    piece = lax.all_gather(right, BOND, axis=0, tiled=True)
    theta = jnp.dot(
        left_three.reshape(local_rows * 2, piece.shape[0]),
        piece,
        preferred_element_type=jnp.float32,
    )
    mixed = apply_gate(theta, pair)
    unused = (jnp.arange(start_basis.shape[1], dtype=jnp.int32) >= rank).astype(jnp.float32)
    basis = start_basis * (1.0 - unused)[None, :]
    for step in range(ITERS):
        image = jnp.dot(mixed, basis, precision=lax.Precision.HIGHEST)
        partial_cols = lax.dot_general(
            mixed, image, (((0,), (0,)), ((), ())), precision=lax.Precision.HIGHEST
        )
        cols = sum_by_parts(partial_cols, (("bond_0", "bond_1"), "bond_2"))
        gram = jnp.dot(cols.T, cols, precision=lax.Precision.HIGHEST) + jnp.diag(unused)
        chol = jnp.linalg.cholesky(gram)
        basis = lax.linalg.triangular_solve(
            chol, cols, left_side=False, lower=True, transpose_a=True
        )
    left_factor = jnp.dot(mixed, basis, precision=lax.Precision.HIGHEST)
    right_factor = jnp.sqrt(jnp.float32(mixed.shape[1])) * basis.T
    return (left_factor, right_factor)


def per_device(last_sites, first_sites, start_basis, fields, ranks):
    segment = lax.axis_index("seg")
    count = lax.axis_size("seg")
    previous = passed_along(last_sites, "seg", 1)
    owner = (segment + count - 1) % count
    left_factor, right_factor = truncate(
        previous[0], first_sites[0], start_basis, fields[owner], ranks[owner]
    )
    new_left = passed_along(left_factor[None], "seg", -1)
    new_right = right_factor[None]
    return (new_left, new_right)


def solution(mesh):
    finer = Mesh(
        mesh.devices.reshape(mesh.shape["seg"], 4, 4, 2), ("seg", "bond_0", "bond_1", "bond_2")
    )
    return jax.shard_map(
        per_device,
        mesh=finer,
        in_specs=(P("seg", BOND, None), P("seg", BOND, None), P(), P(), P()),
        out_specs=(P("seg", BOND, None), P("seg", None, None)),
        check_vma=False,
    )
```

profile of v0, /device:TPU:1, one launch (start us, length us, event | category | flops | bytes accessed | tf_op | source)
XLA Modules:
  0.0 724.9 jit_solution(5119972270818223441)
XLA Ops:
  16.1 59.0 %all-gather.3.cloned.1.call-done = bf16[1,1024,2048]{2,1,0:T(8,128)(2,1)} async-done(((bf16[1,32,2048]{2,1,0:T(8,128)(2,1)}), bf16[1,1024,2048]{2,1,0:T(8,128)(2,1)}) %all-gather.3.cloned.1.call-update) | async-done | bytes 4194320 | tf_op jit(solution)/shard_map/all_gather | solution.py:104
  100.8 34.3 %all_to_all.88 = f32[16,64,256]{2,1,0:T(8,128)} all-to-all(f32[16,64,256]{2,1,0:T(8,128)S(1)} %reduce_sum.72), channel_id=1, replica_groups=mesh['seg'=8,'bond_0'=4,'bond_1'=4,'bond_2'=2] {'bond_0','bond_1'}, dimensions={0} | all-to-all | bytes 2097152 | tf_op jit(solution)/shard_map/all_to_all | solution.py:51
  143.2 23.0 %all-to-all-done.2 = f32[16,64,256]{2,1,0:T(8,128)S(1)} async-done(((f32[16,64,256]{2,1,0:T(8,128)}), f32[16,64,256]{2,1,0:T(8,128)S(1)}, u32[]{:S(2)}, u32[]{:S(2)}) %all-to-all-start.2) | async-done | bytes 1048608 | tf_op jit(solution)/shard_map/all_to_all | solution.py:20
  178.6 11.7 %cholesky.214 = f32[128,128]{1,0:T(8,128)S(1)} custom-call(f32[128,128]{1,0:T(8,128)S(1)} %cholesky.346), custom_call_target="Cholesky" | custom-call | tf_op jit(solution)/shard_map/jit(cholesky)/cholesky | solution.py:120
  200.7 12.1 %cholesky.231 = f32[128,128]{1,0:T(8,128)S(1)} custom-call(f32[128,128]{1,0:T(8,128)S(1)} %convolution_subtract_fusion.7), custom_call_target="Cholesky" | custom-call | tf_op jit(solution)/shard_map/jit(cholesky)/cholesky | solution.py:120
  219.2 19.7 %custom-call.18 = f32[2,128,128]{1,2,0:T(8,128)S(1)} custom-call(f32[2,128,128]{2,1,0:T(8,128)S(1)} %get-tuple-element.30), custom_call_target="InvertDiagBlocksLowerTriangular" | custom-call | tf_op jit(solution)/shard_map/triangular_solve/custom-call.0 | solution.py:121
  256.9 27.8 %all_to_all.89 = f32[16,64,256]{2,1,0:T(8,128)} all-to-all(f32[16,64,256]{2,1,0:T(8,128)S(1)} %reduce_sum.74), channel_id=1, replica_groups=mesh['seg'=8,'bond_0'=4,'bond_1'=4,'bond_2'=2] {'bond_0','bond_1'}, dimensions={0} | all-to-all | bytes 2097152 | tf_op jit(solution)/shard_map/all_to_all | solution.py:51
  294.5 19.9 %all-to-all-done.6 = f32[16,64,256]{2,1,0:T(8,128)S(1)} async-done(((f32[16,64,256]{2,1,0:T(8,128)}), f32[16,64,256]{2,1,0:T(8,128)S(1)}, u32[]{:S(2)}, u32[]{:S(2)}) %all-to-all-start.6) | async-done | bytes 1048608 | tf_op jit(solution)/shard_map/all_to_all | solution.py:20
  314.6 10.1 %all_to_all.83 = f32[2,16,64,256]{3,2,1,0:T(8,128)S(1)} all-to-all(f32[2,16,64,256]{3,2,1,0:T(8,128)S(1)} %broadcast_in_dim.94), channel_id=1, replica_groups=mesh['seg'=8,'bond_0'=4,'bond_1'=4,'bond_2'=2] {'bond_2'}, dimensions={0} | all-to-all | bytes 4194304 | tf_op jit(solution)/shard_map/all_to_all | solution.py:20
  329.6 11.7 %cholesky.248 = f32[128,128]{1,0:T(8,128)S(1)} custom-call(f32[128,128]{1,0:T(8,128)S(1)} %cholesky.349), custom_call_target="Cholesky" | custom-call | tf_op jit(solution)/shard_map/jit(cholesky)/cholesky | solution.py:120
  351.7 12.1 %cholesky.265 = f32[128,128]{1,0:T(8,128)S(1)} custom-call(f32[128,128]{1,0:T(8,128)S(1)} %convolution_subtract_fusion.6), custom_call_target="Cholesky" | custom-call | tf_op jit(solution)/shard_map/jit(cholesky)/cholesky | solution.py:120
  370.2 19.7 %custom-call.20 = f32[2,128,128]{1,2,0:T(8,128)S(1)} custom-call(f32[2,128,128]{2,1,0:T(8,128)S(1)} %get-tuple-element.31), custom_call_target="InvertDiagBlocksLowerTriangular" | custom-call | tf_op jit(solution)/shard_map/triangular_solve/custom-call.0 | solution.py:121
  407.9 32.0 %all_to_all.90 = f32[16,64,256]{2,1,0:T(8,128)} all-to-all(f32[16,64,256]{2,1,0:T(8,128)S(1)} %reduce_sum.76), channel_id=1, replica_groups=mesh['seg'=8,'bond_0'=4,'bond_1'=4,'bond_2'=2] {'bond_0','bond_1'}, dimensions={0} | all-to-all | bytes 2097152 | tf_op jit(solution)/shard_map/all_to_all | solution.py:51
  449.3 18.3 %all-to-all-done.10 = f32[16,64,256]{2,1,0:T(8,128)S(1)} async-done(((f32[16,64,256]{2,1,0:T(8,128)}), f32[16,64,256]{2,1,0:T(8,128)S(1)}, u32[]{:S(2)}, u32[]{:S(2)}) %all-to-all-start.10) | async-done | bytes 1048608 | tf_op jit(solution)/shard_map/all_to_all | solution.py:20
  467.8 11.6 %all_to_all.85 = f32[2,16,64,256]{3,2,1,0:T(8,128)S(1)} all-to-all(f32[2,16,64,256]{3,2,1,0:T(8,128)S(1)} %broadcast_in_dim.96), channel_id=1, replica_groups=mesh['seg'=8,'bond_0'=4,'bond_1'=4,'bond_2'=2] {'bond_2'}, dimensions={0} | all-to-all | bytes 4194304 | tf_op jit(solution)/shard_map/all_to_all | solution.py:20
  484.4 11.7 %cholesky.282 = f32[128,128]{1,0:T(8,128)S(1)} custom-call(f32[128,128]{1,0:T(8,128)S(1)} %cholesky.352), custom_call_target="Cholesky" | custom-call | tf_op jit(solution)/shard_map/jit(cholesky)/cholesky | solution.py:120
  506.4 12.1 %cholesky.299 = f32[128,128]{1,0:T(8,128)S(1)} custom-call(f32[128,128]{1,0:T(8,128)S(1)} %convolution_subtract_fusion.5), custom_call_target="Cholesky" | custom-call | tf_op jit(solution)/shard_map/jit(cholesky)/cholesky | solution.py:120
  524.9 19.7 %custom-call.22 = f32[2,128,128]{1,2,0:T(8,128)S(1)} custom-call(f32[2,128,128]{2,1,0:T(8,128)S(1)} %get-tuple-element.32), custom_call_target="InvertDiagBlocksLowerTriangular" | custom-call | tf_op jit(solution)/shard_map/triangular_solve/custom-call.0 | solution.py:121
  562.6 32.6 %all_to_all.91 = f32[16,64,256]{2,1,0:T(8,128)S(1)} all-to-all(f32[16,64,256]{2,1,0:T(8,128)S(1)} %reduce_sum.78), channel_id=1, replica_groups=mesh['seg'=8,'bond_0'=4,'bond_1'=4,'bond_2'=2] {'bond_0','bond_1'}, dimensions={0} | all-to-all | bytes 2097152 | tf_op jit(solution)/shard_map/all_to_all | solution.py:51
  595.4 24.5 %all_to_all.92 = f32[16,64,256]{2,1,0:T(8,128)S(1)} all-to-all(f32[16,64,256]{2,1,0:T(8,128)S(1)} %broadcast_in_dim.97), channel_id=1, replica_groups=mesh['seg'=8,'bond_0'=4,'bond_1'=4,'bond_2'=2] {'bond_0','bond_1'}, dimensions={0} | all-to-all | bytes 2097152 | tf_op jit(solution)/shard_map/all_to_all | solution.py:20
  620.1 13.9 %all_to_all.87 = f32[2,16,64,256]{3,2,1,0:T(8,128)S(1)} all-to-all(f32[2,16,64,256]{3,2,1,0:T(8,128)S(1)} %broadcast_in_dim.98), channel_id=1, replica_groups=mesh['seg'=8,'bond_0'=4,'bond_1'=4,'bond_2'=2] {'bond_2'}, dimensions={0} | all-to-all | bytes 4194304 | tf_op jit(solution)/shard_map/all_to_all | solution.py:20
  639.0 11.7 %cholesky.316 = f32[128,128]{1,0:T(8,128)S(1)} custom-call(f32[128,128]{1,0:T(8,128)S(1)} %cholesky.355), custom_call_target="Cholesky" | custom-call | tf_op jit(solution)/shard_map/jit(cholesky)/cholesky | solution.py:120
  661.1 11.9 %cholesky.333 = f32[128,128]{1,0:T(8,128)S(1)} custom-call(f32[128,128]{1,0:T(8,128)S(1)} %convolution_subtract_fusion.4), custom_call_target="Cholesky" | custom-call | tf_op jit(solution)/shard_map/jit(cholesky)/cholesky | solution.py:120
  679.7 19.7 %custom-call.24 = f32[2,128,128]{1,2,0:T(8,128)S(1)} custom-call(f32[2,128,128]{2,1,0:T(8,128)S(1)} %get-tuple-element.33), custom_call_target="InvertDiagBlocksLowerTriangular" | custom-call | tf_op jit(solution)/shard_map/triangular_solve/custom-call.0 | solution.py:121
  (175 shorter events, 236.8 us)
Async XLA Ops:
  7.2 3.3 copy-start
  7.2 67.9 %all-gather.3.cloned.1.call-start = ((), (), s32[]{:S(2)}) async-start(), calls=%async_computation.16 | async-start | bytes 4325376 | tf_op jit(solution)/shard_map/all_gather | solution.py:104
  7.9 8.1 %collective-permute-start = (bf16[1,32,2048]{2,1,0:T(8,128)(2,1)}, bf16[1,32,2048]{2,1,0:T(8,128)(2,1)S(1)}, u32[]{:S(2)}, u32[]{:S(2)}) collective-permute-start(bf16[1,32,2048]{2,1,0:T(8,128)(2,1)} %param.8), channel_id=1, source_target_pairs={{0,32},{32,64},{64,96},{96,128},{128,160},{160,192},{192,224},{224... | collective-permute-start | bytes 393224 | tf_op jit(solution)/shard_map/ppermute | solution.py:64
  137.5 28.7 %all-to-all-start.2 = ((f32[16,64,256]{2,1,0:T(8,128)}), f32[16,64,256]{2,1,0:T(8,128)S(1)}, u32[]{:S(2)}, u32[]{:S(2)}) async-start(f32[16,64,256]{2,1,0:T(8,128)} %broadcast_in_dim.89), calls=%async_computation.2 | async-start | bytes 2097152 | tf_op jit(solution)/shard_map/all_to_all | solution.py:20
  173.7 1.3 copy-start.3
  287.1 27.3 %all-to-all-start.6 = ((f32[16,64,256]{2,1,0:T(8,128)}), f32[16,64,256]{2,1,0:T(8,128)S(1)}, u32[]{:S(2)}, u32[]{:S(2)}) async-start(f32[16,64,256]{2,1,0:T(8,128)} %broadcast_in_dim.93), calls=%async_computation.6 | async-start | bytes 2097152 | tf_op jit(solution)/shard_map/all_to_all | solution.py:20
  324.6 1.3 copy-start.4
  442.2 25.3 %all-to-all-start.10 = ((f32[16,64,256]{2,1,0:T(8,128)}), f32[16,64,256]{2,1,0:T(8,128)S(1)}, u32[]{:S(2)}, u32[]{:S(2)}) async-start(f32[16,64,256]{2,1,0:T(8,128)} %broadcast_in_dim.95), calls=%async_computation.10 | async-start | bytes 2097152 | tf_op jit(solution)/shard_map/all_to_all | solution.py:20
  479.4 1.3 copy-start.5
  634.0 1.3 copy-start.2
  705.2 12.6 %copy-start.1 = (f32[8,2]{0,1:T(2,128)S(1)}, f32[8,2]{0,1:T(2,128)}, u32[]{:S(2)}) copy-start(f32[8,2]{0,1:T(2,128)} %param.11) | copy-start | bytes 196
  707.2 10.0 %collective-permute-start.1 = (f32[1,64,256]{2,1,0:T(8,128)S(1)}, f32[1,64,256]{2,1,0:T(8,128)S(1)}, u32[]{:S(2)}, u32[]{:S(2)}) collective-permute-start(f32[1,64,256]{2,1,0:T(8,128)S(1)} %fusion.50), channel_id=1, source_target_pairs={{0,224},{32,0},{64,32},{96,64},{128,96},{160,128},{192,160},{224,1... | collective-permute-start | bytes 196616 | tf_op jit(solution)/shard_map/ppermute | solution.py:64
Sparse Core Ops, SparseCore 0:
  10.5 64.5 all-gather.2
where the time goes:
time: 733 us; the launch traced here: 725 us
  other arithmetic  233 us (32%)
  blocking collectives  219 us (30%)
  waiting for transfers between devices  121 us (17%)
  matrix products  55.6 us (8%)
  local copies, waits for them, and re-layouts  42.7 us (6%)
  starting transfers between devices  30.6 us (4%)
  between operations  22.7 us (3%)
    another operation x28, other arithmetic, truncate(): chol = jnp.linalg.cholesky(gram)  140 us
    all_to_all x4, blocking collectives, sum_by_axis(): lax.all_to_all(nearer, far, split_axis=0, concat_axis=0, tiled=True)  127 us
    another operation x9, other arithmetic, truncate(): lax.linalg.triangular_solve(chol, cols, left_side=False, lower=True, tran...  78.8 us
    all_to_all x5, blocking collectives, sent_to_all(): lax.all_to_all(jnp.broadcast_to(x[None], (peers, *x.shape)), axis, 0, 0,...  67.3 us
    all_to_all x3, waiting for transfers between devices, sent_to_all(): lax.all_to_all(jnp.broadcast_to(x[None], (peers, *x.shape)), axis, 0, 0,...  61.1 us
    all_gather x1, waiting for transfers between devices, truncate(): piece = lax.all_gather(right, BOND, axis=0, tiled=True)  59 us
    all_to_all x4, blocking collectives, sent_and_summed(): pieces = lax.all_to_all(split_up(x, dim, peers), axis, 0, 0, tiled=True)  25.1 us
    all_to_all x3, starting transfers between devices, sent_to_all(): lax.all_to_all(jnp.broadcast_to(x[None], (peers, *x.shape)), axis, 0, 0,...  19.6 us
  transfers between devices with their start and end apart: 6, of which 4 were waited for; matrix products, arithmetic and copies ran while one was open for 1% of the time, Pallas kernels for 0%

commit v1 on v0

--- a/solution.py
+++ b/solution.py
@@ -101,7 +101,9 @@
     local_rows = left.shape[0]
     bond_width = right.shape[1] // 2
     left_three = left.reshape(local_rows, 2, bond_width)
-    piece = lax.all_gather(right, BOND, axis=0, tiled=True)
+    piece = jnp.concatenate(
+        lax.all_to_all(jnp.stack([right] * lax.axis_size(BOND)), BOND, 0, 0), axis=0
+    )
     theta = jnp.dot(
         left_three.reshape(local_rows * 2, piece.shape[0]),
         piece,

time: 733 us -> 768 us (1.048)
  waiting for transfers between devices: 121 us -> 159 us
  between operations: 22.7 us -> 9.23 us
  starting transfers between devices: 30.6 us -> 40.5 us
    ppermute x2, waiting for transfers between devices: 0.01 us -> 91.1 us  [passed_along(): return lax.ppermute(x, axis, [(i, (i + by) % peers) for i in range(peers)])]
    all_gather x1 -> x0, waiting for transfers between devices: 59 us -> none  [truncate(): piece = lax.all_gather(right, BOND, axis=0, tiled=True)]
    all_to_all x0 -> x1, starting transfers between devices: none -> 12.9 us  [truncate(): lax.all_to_all(jnp.stack([right] * lax.axis_size(BOND)), BOND, 0, 0)]
where the time goes in v1:
time: 768 us; the launch traced here: 759 us
  other arithmetic  233 us (30%)
  blocking collectives  216 us (28%)
  waiting for transfers between devices  159 us (21%)
  matrix products  55.6 us (7%)
  local copies, waits for them, and re-layouts  45.5 us (6%)
  starting transfers between devices  40.5 us (5%)
  between operations  9.23 us (1%)
    another operation x28, other arithmetic, truncate(): chol = jnp.linalg.cholesky(gram)  140 us
    all_to_all x4, blocking collectives, sum_by_axis(): lax.all_to_all(nearer, far, split_axis=0, concat_axis=0, tiled=True)  129 us
    ppermute x2, waiting for transfers between devices, passed_along(): return lax.ppermute(x, axis, [(i, (i + by) % peers) for i in range(peers)])  91.1 us
    another operation x9, other arithmetic, truncate(): lax.linalg.triangular_solve(chol, cols, left_side=False, lower=True, tran...  78.8 us
    all_to_all x3, waiting for transfers between devices, sent_to_all(): lax.all_to_all(jnp.broadcast_to(x[None], (peers, *x.shape)), axis, 0, 0,...  68 us
    all_to_all x5, blocking collectives, sent_to_all(): lax.all_to_all(jnp.broadcast_to(x[None], (peers, *x.shape)), axis, 0, 0,...  61.6 us
    all_to_all x4, blocking collectives, sent_and_summed(): pieces = lax.all_to_all(split_up(x, dim, peers), axis, 0, 0, tiled=True)  25.6 us
    all_to_all x3, starting transfers between devices, sent_to_all(): lax.all_to_all(jnp.broadcast_to(x[None], (peers, *x.shape)), axis, 0, 0,...  16.1 us
  transfers between devices with their start and end apart: 6, of which 4 were waited for; matrix products, arithmetic and copies ran while one was open for 1% of the time, Pallas kernels for 0%

profile of v1, /device:TPU:1, one launch (start us, length us, event | category | flops | bytes accessed | tf_op | source)
XLA Modules:
  0.0 759.1 jit_solution(7470822711870439011)
XLA Ops:
  4.1 12.9 %all-to-all-start = ((bf16[32,32,2048]{2,1,0:T(8,128)(2,1)}), bf16[32,32,2048]{2,1,0:T(8,128)(2,1)}, u32[]{:S(2)}, u32[]{:S(2)}) async-start(bf16[32,32,2048]{2,1,0:T(8,128)(2,1)} %stack.46), calls=%async_computation | async-start | bytes 8388608 | tf_op jit(solution)/shard_map/all_to_all | solution.py:105
  22.6 91.1 %collective-permute-done = bf16[1,32,2048]{2,1,0:T(8,128)(2,1)S(1)} collective-permute-done((bf16[1,32,2048]{2,1,0:T(8,128)(2,1)S(1)}, bf16[1,32,2048]{2,1,0:T(8,128)(2,1)S(1)}, u32[]{:S(2)}, u32[]{:S(2)}) %collective-permute-start) | collective-permute-done | bytes 131104 | tf_op jit(solution)/shard_map/ppermute | solution.py:64
  139.9 37.4 %all_to_all.93 = f32[16,64,256]{2,1,0:T(8,128)} all-to-all(f32[16,64,256]{2,1,0:T(8,128)S(1)} %reduce_sum.72), channel_id=1, replica_groups=mesh['seg'=8,'bond_0'=4,'bond_1'=4,'bond_2'=2] {'bond_0','bond_1'}, dimensions={0} | all-to-all | bytes 2097152 | tf_op jit(solution)/shard_map/all_to_all | solution.py:51
  183.9 24.5 %all-to-all-done.3 = f32[16,64,256]{2,1,0:T(8,128)S(1)} async-done(((f32[16,64,256]{2,1,0:T(8,128)}), f32[16,64,256]{2,1,0:T(8,128)S(1)}, u32[]{:S(2)}, u32[]{:S(2)}) %all-to-all-start.3) | async-done | bytes 1048608 | tf_op jit(solution)/shard_map/all_to_all | solution.py:20
  220.8 11.7 %cholesky.214 = f32[128,128]{1,0:T(8,128)S(1)} custom-call(f32[128,128]{1,0:T(8,128)S(1)} %cholesky.346), custom_call_target="Cholesky" | custom-call | tf_op jit(solution)/shard_map/jit(cholesky)/cholesky | solution.py:122
  242.9 12.1 %cholesky.231 = f32[128,128]{1,0:T(8,128)S(1)} custom-call(f32[128,128]{1,0:T(8,128)S(1)} %convolution_subtract_fusion.7), custom_call_target="Cholesky" | custom-call | tf_op jit(solution)/shard_map/jit(cholesky)/cholesky | solution.py:122
  261.5 19.7 %custom-call.18 = f32[2,128,128]{1,2,0:T(8,128)S(1)} custom-call(f32[2,128,128]{2,1,0:T(8,128)S(1)} %get-tuple-element.30), custom_call_target="InvertDiagBlocksLowerTriangular" | custom-call | tf_op jit(solution)/shard_map/triangular_solve/custom-call.0 | solution.py:123
  299.2 31.8 %all_to_all.94 = f32[16,64,256]{2,1,0:T(8,128)} all-to-all(f32[16,64,256]{2,1,0:T(8,128)S(1)} %reduce_sum.74), channel_id=1, replica_groups=mesh['seg'=8,'bond_0'=4,'bond_1'=4,'bond_2'=2] {'bond_0','bond_1'}, dimensions={0} | all-to-all | bytes 2097152 | tf_op jit(solution)/shard_map/all_to_all | solution.py:51
  338.4 23.6 %all-to-all-done.7 = f32[16,64,256]{2,1,0:T(8,128)S(1)} async-done(((f32[16,64,256]{2,1,0:T(8,128)}), f32[16,64,256]{2,1,0:T(8,128)S(1)}, u32[]{:S(2)}, u32[]{:S(2)}) %all-to-all-start.7) | async-done | bytes 1048608 | tf_op jit(solution)/shard_map/all_to_all | solution.py:20
  374.5 11.7 %cholesky.248 = f32[128,128]{1,0:T(8,128)S(1)} custom-call(f32[128,128]{1,0:T(8,128)S(1)} %cholesky.349), custom_call_target="Cholesky" | custom-call | tf_op jit(solution)/shard_map/jit(cholesky)/cholesky | solution.py:122
  396.6 12.1 %cholesky.265 = f32[128,128]{1,0:T(8,128)S(1)} custom-call(f32[128,128]{1,0:T(8,128)S(1)} %convolution_subtract_fusion.6), custom_call_target="Cholesky" | custom-call | tf_op jit(solution)/shard_map/jit(cholesky)/cholesky | solution.py:122
  415.0 19.7 %custom-call.20 = f32[2,128,128]{1,2,0:T(8,128)S(1)} custom-call(f32[2,128,128]{2,1,0:T(8,128)S(1)} %get-tuple-element.31), custom_call_target="InvertDiagBlocksLowerTriangular" | custom-call | tf_op jit(solution)/shard_map/triangular_solve/custom-call.0 | solution.py:123
  452.7 27.7 %all_to_all.95 = f32[16,64,256]{2,1,0:T(8,128)} all-to-all(f32[16,64,256]{2,1,0:T(8,128)S(1)} %reduce_sum.76), channel_id=1, replica_groups=mesh['seg'=8,'bond_0'=4,'bond_1'=4,'bond_2'=2] {'bond_0','bond_1'}, dimensions={0} | all-to-all | bytes 2097152 | tf_op jit(solution)/shard_map/all_to_all | solution.py:51
  490.1 19.9 %all-to-all-done.11 = f32[16,64,256]{2,1,0:T(8,128)S(1)} async-done(((f32[16,64,256]{2,1,0:T(8,128)}), f32[16,64,256]{2,1,0:T(8,128)S(1)}, u32[]{:S(2)}, u32[]{:S(2)}) %all-to-all-start.11) | async-done | bytes 1048608 | tf_op jit(solution)/shard_map/all_to_all | solution.py:20
  525.3 11.7 %cholesky.282 = f32[128,128]{1,0:T(8,128)S(1)} custom-call(f32[128,128]{1,0:T(8,128)S(1)} %cholesky.352), custom_call_target="Cholesky" | custom-call | tf_op jit(solution)/shard_map/jit(cholesky)/cholesky | solution.py:122
  547.3 12.1 %cholesky.299 = f32[128,128]{1,0:T(8,128)S(1)} custom-call(f32[128,128]{1,0:T(8,128)S(1)} %convolution_subtract_fusion.5), custom_call_target="Cholesky" | custom-call | tf_op jit(solution)/shard_map/jit(cholesky)/cholesky | solution.py:122
  565.8 19.7 %custom-call.22 = f32[2,128,128]{1,2,0:T(8,128)S(1)} custom-call(f32[2,128,128]{2,1,0:T(8,128)S(1)} %get-tuple-element.32), custom_call_target="InvertDiagBlocksLowerTriangular" | custom-call | tf_op jit(solution)/shard_map/triangular_solve/custom-call.0 | solution.py:123
  603.5 31.9 %all_to_all.96 = f32[16,64,256]{2,1,0:T(8,128)S(1)} all-to-all(f32[16,64,256]{2,1,0:T(8,128)S(1)} %reduce_sum.78), channel_id=1, replica_groups=mesh['seg'=8,'bond_0'=4,'bond_1'=4,'bond_2'=2] {'bond_0','bond_1'}, dimensions={0} | all-to-all | bytes 2097152 | tf_op jit(solution)/shard_map/all_to_all | solution.py:51
  635.6 24.8 %all_to_all.97 = f32[16,64,256]{2,1,0:T(8,128)S(1)} all-to-all(f32[16,64,256]{2,1,0:T(8,128)S(1)} %broadcast_in_dim.97), channel_id=1, replica_groups=mesh['seg'=8,'bond_0'=4,'bond_1'=4,'bond_2'=2] {'bond_0','bond_1'}, dimensions={0} | all-to-all | bytes 2097152 | tf_op jit(solution)/shard_map/all_to_all | solution.py:20
  660.6 12.3 %all_to_all.92 = f32[2,16,64,256]{3,2,1,0:T(8,128)S(1)} all-to-all(f32[2,16,64,256]{3,2,1,0:T(8,128)S(1)} %broadcast_in_dim.98), channel_id=1, replica_groups=mesh['seg'=8,'bond_0'=4,'bond_1'=4,'bond_2'=2] {'bond_2'}, dimensions={0} | all-to-all | bytes 4194304 | tf_op jit(solution)/shard_map/all_to_all | solution.py:20
  677.9 11.7 %cholesky.316 = f32[128,128]{1,0:T(8,128)S(1)} custom-call(f32[128,128]{1,0:T(8,128)S(1)} %cholesky.355), custom_call_target="Cholesky" | custom-call | tf_op jit(solution)/shard_map/jit(cholesky)/cholesky | solution.py:122
  700.0 11.9 %cholesky.333 = f32[128,128]{1,0:T(8,128)S(1)} custom-call(f32[128,128]{1,0:T(8,128)S(1)} %convolution_subtract_fusion.4), custom_call_target="Cholesky" | custom-call | tf_op jit(solution)/shard_map/jit(cholesky)/cholesky | solution.py:122
  718.6 19.7 %custom-call.24 = f32[2,128,128]{1,2,0:T(8,128)S(1)} custom-call(f32[2,128,128]{2,1,0:T(8,128)S(1)} %get-tuple-element.33), custom_call_target="InvertDiagBlocksLowerTriangular" | custom-call | tf_op jit(solution)/shard_map/triangular_solve/custom-call.0 | solution.py:123
  746.1 10.6 %collective-permute-start.1 = (f32[1,64,256]{2,1,0:T(8,128)S(1)}, f32[1,64,256]{2,1,0:T(8,128)S(1)}, u32[]{:S(2)}, u32[]{:S(2)}) collective-permute-start(f32[1,64,256]{2,1,0:T(8,128)S(1)} %fusion.50), channel_id=1, source_target_pairs={{0,224},{32,0},{64,32},{96,64},{128,96},{160,128},{192,160},{224,1... | collective-permute-start | bytes 196616 | tf_op jit(solution)/shard_map/ppermute | solution.py:64
  (179 shorter events, 242.9 us)
Async XLA Ops:
  0.6 17.2 %copy-start = (f32[8,2]{0,1:T(2,128)S(1)}, f32[8,2]{0,1:T(2,128)}, u32[]{:S(2)}) copy-start(f32[8,2]{0,1:T(2,128)} %param.11) | copy-start | bytes 196
  4.0 12.9 %copy-start.6 = (bf16[1,32,2048]{2,1,0:T(8,128)(2,1)S(1)}, bf16[1,32,2048]{2,1,0:T(8,128)(2,1)}, u32[]{:S(2)}) copy-start(bf16[1,32,2048]{2,1,0:T(8,128)(2,1)} %param.8) | copy-start | bytes 393220
  4.1 17.4 %copy-start.7 = (s32[8]{0:T(128)S(1)}, s32[8]{0:T(128)}, u32[]{:S(2)}) copy-start(s32[8]{0:T(128)} %param.12) | copy-start | bytes 100
  4.1 109.7 %all-to-all-start = ((bf16[32,32,2048]{2,1,0:T(8,128)(2,1)}), bf16[32,32,2048]{2,1,0:T(8,128)(2,1)}, u32[]{:S(2)}, u32[]{:S(2)}) async-start(bf16[32,32,2048]{2,1,0:T(8,128)(2,1)} %stack.46), calls=%async_computation | async-start | bytes 8388608 | tf_op jit(solution)/shard_map/all_to_all | solution.py:105
  17.0 96.7 %collective-permute-start = (bf16[1,32,2048]{2,1,0:T(8,128)(2,1)S(1)}, bf16[1,32,2048]{2,1,0:T(8,128)(2,1)S(1)}, u32[]{:S(2)}, u32[]{:S(2)}) collective-permute-start(bf16[1,32,2048]{2,1,0:T(8,128)(2,1)S(1)} %copy-done.6), channel_id=1, source_target_pairs={{0,32},{32,64},{64,96},{96,128},{128,160},{160,192},{192,224},{224... | collective-permute-start | bytes 393224 | tf_op jit(solution)/shard_map/ppermute | solution.py:64
  179.6 28.7 %all-to-all-start.3 = ((f32[16,64,256]{2,1,0:T(8,128)}), f32[16,64,256]{2,1,0:T(8,128)S(1)}, u32[]{:S(2)}, u32[]{:S(2)}) async-start(f32[16,64,256]{2,1,0:T(8,128)} %broadcast_in_dim.89), calls=%async_computation.3 | async-start | bytes 2097152 | tf_op jit(solution)/shard_map/all_to_all | solution.py:20
  215.9 1.3 copy-start.3
  333.3 28.7 %all-to-all-start.7 = ((f32[16,64,256]{2,1,0:T(8,128)}), f32[16,64,256]{2,1,0:T(8,128)S(1)}, u32[]{:S(2)}, u32[]{:S(2)}) async-start(f32[16,64,256]{2,1,0:T(8,128)} %broadcast_in_dim.93), calls=%async_computation.7 | async-start | bytes 2097152 | tf_op jit(solution)/shard_map/all_to_all | solution.py:20
  369.5 1.3 copy-start.4
  482.8 27.2 %all-to-all-start.11 = ((f32[16,64,256]{2,1,0:T(8,128)}), f32[16,64,256]{2,1,0:T(8,128)S(1)}, u32[]{:S(2)}, u32[]{:S(2)}) async-start(f32[16,64,256]{2,1,0:T(8,128)} %broadcast_in_dim.95), calls=%async_computation.11 | async-start | bytes 2097152 | tf_op jit(solution)/shard_map/all_to_all | solution.py:20
  520.3 1.3 copy-start.5
  672.9 1.3 copy-start.2
  744.1 14.8 %copy-start.1 = (f32[8,2]{0,1:T(2,128)S(1)}, f32[8,2]{0,1:T(2,128)}, u32[]{:S(2)}) copy-start(f32[8,2]{0,1:T(2,128)} %param.11) | copy-start | bytes 196
  746.1 12.1 %collective-permute-start.1 = (f32[1,64,256]{2,1,0:T(8,128)S(1)}, f32[1,64,256]{2,1,0:T(8,128)S(1)}, u32[]{:S(2)}, u32[]{:S(2)}) collective-permute-start(f32[1,64,256]{2,1,0:T(8,128)S(1)} %fusion.50), channel_id=1, source_target_pairs={{0,224},{32,0},{64,32},{96,64},{128,96},{160,128},{192,160},{224,1... | collective-permute-start | bytes 196616 | tf_op jit(solution)/shard_map/ppermute | solution.py:64
